TPU v7x, 32 devices: a whole 2x2x4 slice. The times are simulated.
32 devices in a mesh: dp: 2 (over x), seq: 16 (over z, y, core).
Axes of the slice: x: 2, y: 2, z: 4, core: 2. Of those that a mesh axis runs over, the one named last changes fastest.
Arguments:
- pixels: bfloat16 [4096, 768], P(('dp', 'seq')), may hold values from -6 to 6
- mask: int32 [4096], P(('dp', 'seq')), may hold values 0 or 1
- image_count: int32 [2, 6], P('dp'), may hold values from 1 to 1024, 2048 in all within a row
- image_width: int32 [2, 6], P('dp'), may hold values from 4 to 63
- gsd_index: int32 [2, 6], P('dp'), may hold values from 0 to 8
- step: int32 [1], replicated, may hold values from 2 to 20
- master: float32 [17551360], P(('dp', 'seq')), as said below
- moment_one: float32 [17551360], P(('dp', 'seq')), as said below
- moment_two: float32 [17551360], P(('dp', 'seq')), as said below
Outputs:
- new_master: float32 [17551360], P(('dp', 'seq'))
- new_moment_one: float32 [17551360], P(('dp', 'seq'))
- new_moment_two: float32 [17551360], P(('dp', 'seq'))
- loss: float32 [1], replicated
- grad_norm: float32 [1], replicated
Inputs may be any that keep to these rules, and one draw needn't show every extreme that they name: master holds each weight drawn by its fan-in, gains near 1. moment_two is positive. moment_one takes both signs.
All inputs are finite; a program needn't handle non-finite values. No bound on the sum of `mask` on one device may be relied on, other than what follows from the above.
Results may differ from a plain program's by a relative error of at most 0.0024.
The roundings to bfloat16 on the way count: a program that leaves them out, or rounds other values in their place, can miss the bound.
Values may be sent and summed in bfloat16 or wider, within the bound.
A program may use at most 512 MiB of HBM per device.

v0:
```python
import math

import jax
import jax.numpy as jnp
from jax import lax
from jax.sharding import PartitionSpec as P

D = 1024
HEADS = 16
FF = 4096
DD = 512
DHEADS = 16
DFF = 2048
PATCH = 16
PIX = 768
LOWPIX = 192


clip_level = 0.0001
peak_rate = 0.1
warm_steps = 10.0
decay_rate = 0.05
adam_eps = 1e-12


def param_shapes():
    return [
        (PIX, D),
        (D,),
        (4, D),
        (D, 3 * D),
        (D, D),
        (D,),
        (D, FF),
        (FF,),
        (FF, D),
        (D,),
        (D, DD),
        (DD,),
        (DD,),
        (4, DD),
        (DD, 3 * DD),
        (DD, DD),
        (DD,),
        (DD, DFF),
        (DFF,),
        (DFF, DD),
        (DD,),
        (DD, PIX),
        (PIX,),
        (DD, LOWPIX),
        (LOWPIX,),
    ]


def unpack(flat):
    pieces = []
    offset = 0
    for shape in param_shapes():
        length = math.prod(shape)
        pieces.append(lax.slice_in_dim(flat, offset, offset + length).reshape(shape))
        offset += length
    return pieces


def matmul(a, b):
    return jnp.dot(a, b, preferred_element_type=jnp.float32)


def outer(a, b):
    return lax.dot_general(a, b, (((0,), (0,)), ((), ())), preferred_element_type=jnp.float32)


def back_mul(a, weight):
    return lax.dot_general(a, weight, (((1,), (1,)), ((), ())), preferred_element_type=jnp.float32)


def layer_norm(x, gain, shift):
    centred = x - jnp.mean(x, axis=-1, keepdims=True)
    return (
        centred * lax.rsqrt(jnp.mean(centred * centred, axis=-1, keepdims=True) + 1e-06) * gain
        + shift
    )


def geometry(counts, widths, ground, places):
    ends = jnp.cumsum(counts)
    starts = ends - counts
    inside = ((places[:, None] >= starts[None, :]) & (places[:, None] < ends[None, :])).astype(
        jnp.int32
    )
    image = jnp.sum(inside * jnp.arange(counts.shape[0], dtype=jnp.int32)[None, :], axis=1)
    start = jnp.sum(inside * starts[None, :], axis=1)
    width = jnp.sum(inside * widths[None, :], axis=1)
    level = jnp.sum(inside * ground[None, :], axis=1)
    local = places - start
    row_num = local // width
    col_num = local - row_num * width
    ratio = jnp.exp2(level.astype(jnp.float32) * 0.25)
    return (image, local, row_num.astype(jnp.float32) * ratio, col_num.astype(jnp.float32) * ratio)


def position_code(row_pos, col_pos, width):
    quarter = width // 4
    freqs = jnp.power(10000.0, -jnp.arange(quarter, dtype=jnp.float32) / quarter)
    row_ang = row_pos[:, None] * freqs[None, :]
    col_ang = col_pos[:, None] * freqs[None, :]
    return jnp.concatenate(
        [jnp.sin(row_ang), jnp.cos(row_ang), jnp.sin(col_ang), jnp.cos(col_ang)], axis=1
    )


def pool_table():
    values = 3 * PATCH * PATCH
    index = jnp.arange(values, dtype=jnp.int32)
    channel = index % 3
    cell = index // 3
    row_num = cell // PATCH
    col_num = cell % PATCH
    target = (row_num // 2 * (PATCH // 2) + col_num // 2) * 3 + channel
    return (target[:, None] == jnp.arange(values // 4, dtype=jnp.int32)[None, :]).astype(
        jnp.float32
    ) * 0.25


def masked_scores(queries, keys, query_image, key_image, key_seen, scale):
    raw = jnp.einsum("rhd,khd->hrk", queries, keys, preferred_element_type=jnp.float32) * scale
    allowed = (query_image[:, None] == key_image[None, :]) & (key_seen[None, :] > 0)
    return jnp.where(allowed[None], raw, -1e30)


def attend(queries, keys, values, key_seen, query_image, key_image, scale):
    scores = masked_scores(queries, keys, query_image, key_image, key_seen, scale)
    top = jnp.max(scores, axis=-1)
    mass = jnp.sum(jnp.where(scores > -1e29, jnp.exp(scores - top[..., None]), 0.0), axis=-1)
    lse = top + jnp.log(mass)
    probs = jnp.exp(scores - lse[..., None]).astype(jnp.bfloat16)
    out = jnp.einsum("hrk,khd->rhd", probs, values, preferred_element_type=jnp.float32)
    return (out, lse)


def attend_back(queries, keys, values, key_seen, query_image, key_image, out, lse, grad_out, scale):
    rows, heads, depth = queries.shape
    dterm = jnp.transpose(jnp.sum(grad_out.astype(jnp.float32) * out, axis=-1))
    scores = masked_scores(queries, keys, query_image, key_image, key_seen, scale)
    probs = jnp.exp(scores - lse[..., None])
    dprob = jnp.einsum("rhd,khd->hrk", grad_out, values, preferred_element_type=jnp.float32)
    dscore = (probs * (dprob - dterm[..., None])).astype(jnp.bfloat16)
    probs_low = probs.astype(jnp.bfloat16)
    grad_queries = jnp.einsum("hrk,khd->rhd", dscore, keys, preferred_element_type=jnp.float32)
    count = rows * lax.axis_size("seq")
    grad_keys = (
        jnp.einsum("hrk,rhd->khd", dscore, queries, preferred_element_type=jnp.float32) * scale
    )
    grad_values = jnp.einsum(
        "hrk,rhd->khd", probs_low, grad_out, preferred_element_type=jnp.float32
    )
    grad_kv = lax.psum_scatter(
        jnp.concatenate([grad_keys.reshape(count, -1), grad_values.reshape(count, -1)], axis=1),
        "seq",
        scatter_dimension=0,
        tiled=True,
    )
    return (grad_queries * scale, grad_kv)


def block_forward(x, weights, seen, query_image, key_image, heads):
    norms, qkv_w, out_w, out_b, up_w, up_b, down_w, down_b = weights
    gains = norms.astype(jnp.float32)
    rows, width = x.shape
    depth = width // heads
    scale = depth ** (-0.5)
    normed = layer_norm(x, gains[0], gains[1]).astype(jnp.bfloat16)
    mixed = matmul(normed, qkv_w).astype(jnp.bfloat16)
    queries = mixed[:, :width].reshape(rows, heads, depth)
    all_keys, all_values, all_seen = (
        lax.all_gather(mixed[:, width : 2 * width], "seq", axis=0, tiled=True),
        lax.all_gather(mixed[:, 2 * width :], "seq", axis=0, tiled=True),
        lax.all_gather(seen, "seq", axis=0, tiled=True),
    )
    all_keys = all_keys.reshape(-1, heads, depth)
    all_values = all_values.reshape(-1, heads, depth)
    out, lse = attend(queries, all_keys, all_values, all_seen, query_image, key_image, scale)
    attended = out.reshape(rows, width).astype(jnp.bfloat16)
    resid = x + matmul(attended, out_w) + out_b.astype(jnp.float32)
    normed_two = layer_norm(resid, gains[2], gains[3]).astype(jnp.bfloat16)
    pre = matmul(normed_two, up_w) + up_b.astype(jnp.float32)
    hidden_act = jax.nn.gelu(pre, approximate=False).astype(jnp.bfloat16)
    result = resid + matmul(hidden_act, down_w) + down_b.astype(jnp.float32)
    kept = (
        x,
        normed,
        queries,
        all_keys,
        all_values,
        all_seen,
        out,
        lse,
        attended,
        resid,
        normed_two,
        pre,
        hidden_act,
    )
    return (result, kept)


def block_backward(grad, weights, kept, query_image, key_image, heads):
    norms, qkv_w, out_w, out_b, up_w, up_b, down_w, down_b = weights
    gains = norms.astype(jnp.float32)
    (
        x,
        normed,
        queries,
        all_keys,
        all_values,
        all_seen,
        out,
        lse,
        attended,
        resid,
        normed_two,
        pre,
        hidden_act,
    ) = kept
    rows, width = x.shape
    depth = width // heads
    grad_low = grad.astype(jnp.bfloat16)
    grad_down = outer(hidden_act, grad_low)
    grad_down_b = jnp.sum(grad, axis=0)
    _, gelu_back = jax.vjp(lambda value: jax.nn.gelu(value, approximate=False), pre)
    (grad_pre,) = gelu_back(back_mul(grad_low, down_w))
    pre_low = grad_pre.astype(jnp.bfloat16)
    grad_up = outer(normed_two, pre_low)
    grad_up_b = jnp.sum(grad_pre, axis=0)
    _, norm_two_back = jax.vjp(layer_norm, resid, gains[2], gains[3])
    grad_resid, grad_gain_two, grad_shift_two = norm_two_back(back_mul(pre_low, up_w))
    grad_resid = grad_resid + grad
    resid_low = grad_resid.astype(jnp.bfloat16)
    grad_out = outer(attended, resid_low)
    grad_out_b = jnp.sum(grad_resid, axis=0)
    grad_attended = back_mul(resid_low, out_w).astype(jnp.bfloat16).reshape(rows, heads, depth)
    grad_queries, grad_kv = attend_back(
        queries,
        all_keys,
        all_values,
        all_seen,
        query_image,
        key_image,
        out,
        lse,
        grad_attended,
        depth ** (-0.5),
    )
    mixed_low = jnp.concatenate([grad_queries.reshape(rows, width), grad_kv], axis=1).astype(
        jnp.bfloat16
    )
    grad_qkv = outer(normed, mixed_low)
    _, norm_one_back = jax.vjp(layer_norm, x, gains[0], gains[1])
    grad_x, grad_gain_one, grad_shift_one = norm_one_back(back_mul(mixed_low, qkv_w))
    grad_norms = jnp.stack([grad_gain_one, grad_shift_one, grad_gain_two, grad_shift_two])
    return (
        grad_x + grad_resid,
        [grad_norms, grad_qkv, grad_out, grad_out_b, grad_up, grad_up_b, grad_down, grad_down_b],
    )


def body(pixels, mask, image_count, image_width, gsd_index, step, master, moment_one, moment_two):
    flat = lax.all_gather(master.astype(jnp.bfloat16), ("dp", "seq"), axis=0, tiled=True)
    weights = unpack(flat)
    rows = pixels.shape[0]
    group_rows = rows * lax.axis_size("seq")
    places = lax.axis_index("seq") * rows + jnp.arange(rows, dtype=jnp.int32)
    counts, widths, ground = (image_count[0], image_width[0], gsd_index[0])
    query_image, local, row_pos, col_pos = geometry(counts, widths, ground, places)
    key_image = geometry(counts, widths, ground, jnp.arange(group_rows, dtype=jnp.int32))[0]
    hidden = ((mask == 1) & (local != 0)).astype(jnp.float32)
    count_local = jnp.sum(hidden)
    count = lax.psum(count_local, ("dp", "seq"))
    embedded = (
        matmul(pixels, weights[0])
        + weights[1].astype(jnp.float32)
        + position_code(row_pos, col_pos, D)
    )
    encoded, enc_kept = block_forward(
        embedded, weights[2:10], (1.0 - hidden).astype(jnp.bfloat16), query_image, key_image, HEADS
    )
    encoded_low = encoded.astype(jnp.bfloat16)
    projected = matmul(encoded_low, weights[10]) + weights[11].astype(jnp.float32)
    dec_in = jnp.where(
        hidden[:, None] > 0, weights[12].astype(jnp.float32)[None, :], projected
    ) + position_code(row_pos, col_pos, DD)
    decoded, dec_kept = block_forward(
        dec_in, weights[13:21], jnp.ones((rows,), jnp.bfloat16), query_image, key_image, DHEADS
    )
    decoded_low = decoded.astype(jnp.bfloat16)
    high = matmul(decoded_low, weights[21]) + weights[22].astype(jnp.float32)
    low_pred = matmul(decoded_low, weights[23]) + weights[24].astype(jnp.float32)
    table = pool_table()
    pix_wide = pixels.astype(jnp.float32)
    low_target = jnp.dot(
        pix_wide, table, precision=lax.Precision.HIGHEST, preferred_element_type=jnp.float32
    )
    high_target = pix_wide - jnp.dot(
        low_target,
        4.0 * table.T,
        precision=lax.Precision.HIGHEST,
        preferred_element_type=jnp.float32,
    )
    per_patch = jnp.mean(jnp.abs(high - high_target), axis=-1) + jnp.mean(
        (low_pred - low_target) ** 2, axis=-1
    )
    loss_local = jnp.sum(hidden * per_patch)
    grad_high = hidden[:, None] * jnp.sign(high - high_target) / PIX
    grad_low_pred = hidden[:, None] * 2.0 * (low_pred - low_target) / LOWPIX
    high_low = grad_high.astype(jnp.bfloat16)
    lowband_low = grad_low_pred.astype(jnp.bfloat16)
    grad_decoded = back_mul(high_low, weights[21]) + back_mul(lowband_low, weights[23])
    grad_dec_in, dec_grads = block_backward(
        grad_decoded, weights[13:21], dec_kept, query_image, key_image, DHEADS
    )
    grad_token = jnp.sum(hidden[:, None] * grad_dec_in, axis=0)
    grad_projected = grad_dec_in * (1.0 - hidden)[:, None]
    projected_low = grad_projected.astype(jnp.bfloat16)
    grad_encoded = back_mul(projected_low, weights[10])
    grad_embedded, enc_grads = block_backward(
        grad_encoded, weights[2:10], enc_kept, query_image, key_image, HEADS
    )
    grads = (
        [outer(pixels, grad_embedded.astype(jnp.bfloat16)), jnp.sum(grad_embedded, axis=0)]
        + enc_grads
        + [outer(encoded_low, projected_low), jnp.sum(grad_projected, axis=0), grad_token]
        + dec_grads
        + [
            outer(decoded_low, high_low),
            jnp.sum(grad_high, axis=0),
            outer(decoded_low, lowband_low),
            jnp.sum(grad_low_pred, axis=0),
        ]
    )
    shard = master.shape[0]
    groups, seqs = (lax.axis_size("dp"), lax.axis_size("seq"))
    total_params = shard * groups * seqs
    used = sum((math.prod(shape) for shape in param_shapes()))
    grad_flat = jnp.concatenate(
        [g.reshape(-1) for g in grads] + [jnp.zeros((total_params - used,), jnp.float32)]
    )
    partial_share = lax.psum_scatter(
        grad_flat.reshape(groups, seqs, shard), "seq", scatter_dimension=1, tiled=True
    )
    summed = lax.psum(partial_share, "dp")
    owned = lax.dynamic_index_in_dim(summed, lax.axis_index("dp"), 0, keepdims=False)[0]
    square_sum = jnp.sum(owned * owned)
    loss_total, square_total = lax.psum((loss_local, square_sum), ("dp", "seq"))
    grad_norm = jnp.sqrt(square_total) / count
    clipped = owned * (jnp.minimum(1.0, clip_level / grad_norm) / count)
    first = 0.5 * moment_one + 0.5 * clipped
    second = 0.5 * moment_two + 0.5 * clipped * clipped
    step_value = step[0].astype(jnp.float32)
    correction = 1.0 - jnp.power(0.5, step_value)
    rate = peak_rate * jnp.minimum(1.0, step_value / warm_steps)
    new_master = master - rate * (
        first / correction / (jnp.sqrt(second / correction) + adam_eps) + decay_rate * master
    )
    return (new_master, first, second, (loss_total / count).reshape(1), grad_norm.reshape(1))


def solution(mesh):
    in_specs = (
        P(("dp", "seq"), None),
        P(("dp", "seq")),
        P("dp", None),
        P("dp", None),
        P("dp", None),
        P(),
        P(("dp", "seq")),
        P(("dp", "seq")),
        P(("dp", "seq")),
    )
    out_specs = (P(("dp", "seq")), P(("dp", "seq")), P(("dp", "seq")), P(), P())
    return jax.shard_map(body, mesh=mesh, in_specs=in_specs, out_specs=out_specs, check_vma=False)
```

profile of v0, /device:TPU:0, one launch (start us, length us, event | category | flops | bytes accessed | tf_op | source)
XLA Modules:
  0.0 3450.0 jit_solution(14075039186222475328)
XLA Ops:
  9.0 13.2 reshape.656
  23.9 23.2 all-gather.1
  50.9 345.3 %all-gather.16.cloned.1.call-done = bf16[32,1,548480]{2,1,0:T(2,128)(2,1)} async-done(((bf16[1,1,548480]{2,1,0:T(2,128)(2,1)}), bf16[32,1,548480]{2,1,0:T(2,128)(2,1)}) %all-gather.16.cloned.1.call-update) | async-done | bytes 35102736 | tf_op jit(solution)/shard_map/all_gather | solution.py:269
  396.2 220.1 %reduce.1 = bf16[32,548480]{1,0:T(8,128)(2,1)} reduce(bf16[32,1,548480]{2,1,0:T(2,128)(2,1)} %all-gather.16.cloned.1.call-done, bf16[]{:T(256)} %constant.289), dimensions={1}, to_apply=%all-gather.reduce_sub_computation | reduce | bytes 70205440 | tf_op jit(solution)/shard_map/all_gather | solution.py:269
  616.3 80.3 %reshape.657 = bf16[17551360]{0:T(1024)(128)(2,1)} reshape(bf16[32,548480]{1,0:T(8,128)(2,1)} %reduce.1) | data formatting | bytes 70205440
  713.4 10.3 reshape.611
  728.5 11.4 fusion.139
  749.3 13.5 reshape.615
  762.7 13.5 slice.224
  791.8 10.9 fusion.2
  802.7 9.7 fusion.4
  835.5 12.1 fusion.146
  876.1 25.4 all-gather.12.cloned.1.call-done
  905.4 10.4 fusion.3
  915.8 9.4 fusion.5
  925.2 9.4 select_reduce_fusion
  947.9 11.3 fusion.149
  972.0 12.7 fusion.67
  984.7 9.7 multiply_convert_fusion.1
  1011.5 96.6 %reduce-scatter.3.cloned.1.call-done = f32[128,1024]{0,1:T(8,128)} async-done(((f32[2048,1024]{0,1:T(8,128)}), f32[128,1024]{0,1:T(8,128)}) %reduce-scatter.3.cloned.1.call-update) | async-done | bytes 524304 | tf_op jit(solution)/shard_map/reduce_scatter | solution.py:158
  1111.5 10.5 fusion.151
  1129.5 10.2 fusion.64
  1139.6 10.7 multiply_convert_fusion
  1221.6 120.0 %reduce-scatter.5.cloned.1.call-done = f32[128,2048]{0,1:T(8,128)} async-done(((f32[2048,2048]{0,1:T(8,128)}), f32[128,2048]{0,1:T(8,128)}) %reduce-scatter.5.cloned.1.call-update) | async-done | bytes 1048592 | tf_op jit(solution)/shard_map/reduce_scatter | solution.py:158
  1358.0 12.3 copy.76
  1378.0 545.7 %concatenate.29 = f32[17551360]{0:T(1024)} concatenate(f32[786432]{0:T(1024)} %bitcast.185, f32[1024]{0:T(1024)} %get-tuple-element.14, f32[4096]{0:T(1024)S(1)} %bitcast.210, f32[3145728]{0:T(1024)} %bitcast.173, f32[1048576]{0:T(1024)} %bitcast.182, f32[1024]{0:T(1024)} %get-tuple-element.13, f32[4194304]{0:T(1024)} %bitcast.169, f32[4096]{0:T(1024)} %get-tuple-element.129, ...), dimensions={0} | concatenate | bytes 140410880 | tf_op jit(solution)/shard_map/concatenate | solution.py:345
  1923.7 68.2 %reshape.653 = f32[2,16,548480]{2,1,0:T(8,128)} reshape(f32[17551360]{0:T(1024)} %concatenate.29) | data formatting | bytes 140410880 | tf_op jit(solution)/shard_map/reshape | solution.py:349
  1991.9 113.0 %copy.72 = f32[2,16,548480]{2,0,1:T(2,128)} copy(f32[2,16,548480]{2,1,0:T(8,128)} %reshape.653) | data formatting | bytes 140410880 | tf_op jit(solution)/shard_map/reshape | solution.py:349
  2106.1 1137.4 %all-reduce.7.cloned.1.call-done = f32[2,16,548480]{2,0,1:T(2,128)} async-done(((f32[2,16,548480]{2,0,1:T(2,128)}), f32[2,16,548480]{2,0,1:T(2,128)}) %all-reduce.7.cloned.1.call-update) | async-done | bytes 70205456
  3251.6 110.4 %all-reduce.5.cloned.1.call-done = f32[2,1,548480]{2,0,1:T(2,128)} async-done(((f32[2,1,548480]{2,0,1:T(2,128)}), f32[2,1,548480]{2,0,1:T(2,128)}) %all-reduce.5.cloned.1.call-update) | async-done | bytes 4387856 | tf_op jit(solution)/shard_map/psum | solution.py:351
  3368.9 39.9 %all-reduce.1 = (f32[]{:T(128)}, f32[]{:T(128)}, f32[]{:T(128)}) all-reduce(f32[]{:T(128)} %get-tuple-element.30, f32[]{:T(128)} %multiply_reduce_fusion.1, f32[]{:T(128)} %get-tuple-element.29), channel_id=1, replica_groups=mesh['dp'=2,'seq'=16] {'dp','seq'}, use_global_device_ids=true, to_apply=%region_52.53 | all-reduce | flops 3 | bytes 24 | tf_op jit(solution)/shard_map/psum | solution.py:279
  3412.9 24.0 multiply_reduce_fusion
  (397 shorter events, 276.1 us)
Async XLA Ops:
  7.2 389.1 %all-gather.16.cloned.1.call-start = ((), (), s32[]{:S(2)}) async-start(), calls=%async_computation.9 | async-start | bytes 72399360 | tf_op jit(solution)/shard_map/all_gather | solution.py:269
  9.0 13.6 copy-start.91
  9.0 13.6 copy-start.92
  9.0 13.8 copy-start.93
  22.3 763.0 %all-gather.8.cloned.1.call-start = ((), (), s32[]{:S(2)}) async-start(), calls=%async_computation.2 | async-start | bytes 4456448 | tf_op jit(solution)/shard_map/all_gather | solution.py:177
  23.3 23.9 copy-start.87
  712.5 135.1 %copy-start.5 = (f32[128,1024]{1,0:T(8,128)}, f32[128,1024]{1,0:T(8,128)S(1)}, u32[]{:S(2)}) copy-start(f32[128,1024]{1,0:T(8,128)S(1)} %get-tuple-element.109) | copy-start | bytes 1572868
  728.5 100.1 %all-gather.10.cloned.1.call-start = ((), (), s32[]{:S(2)}) async-start(), calls=%async_computation.3 | async-start | bytes 4456448 | tf_op jit(solution)/shard_map/all_gather | solution.py:178
  739.9 161.6 %all-gather.12.cloned.1.call-start = ((), (), s32[]{:S(2)}) async-start(), calls=%async_computation.4 | async-start | bytes 2228224 | tf_op jit(solution)/shard_map/all_gather | solution.py:177
  747.0 44.8 %copy-start.20 = (bf16[128,1024]{0,1:T(8,128)(2,1)}, bf16[128,1024]{0,1:T(8,128)(2,1)S(1)}, u32[]{:S(2)}) copy-start(bf16[128,1024]{0,1:T(8,128)(2,1)S(1)} %copy.63) | copy-start | bytes 786436
  762.7 13.5 slice-start
  821.8 13.7 copy-start.64
  835.5 15.3 slice-start.3
  835.5 15.3 slice-start.4
  861.5 82.3 %all-gather.14.cloned.1.call-start = ((), (), s32[]{:S(2)}) async-start(), calls=%async_computation.5 | async-start | bytes 2228224 | tf_op jit(solution)/shard_map/all_gather | solution.py:178
  863.6 244.5 %reduce-scatter.3.cloned.1.call-start = ((), (), s32[]{:S(2)}) async-start(), calls=%async_computation.6 | async-start | bytes 8912896 | tf_op jit(solution)/shard_map/reduce_scatter | solution.py:158
  876.1 29.3 copy-start.12
  1004.4 104.9 %copy-start.14 = (bf16[512,1536]{1,0:T(8,128)(2,1)S(1)}, bf16[512,1536]{1,0:T(8,128)(2,1)}, u32[]{:S(2)}) copy-start(bf16[512,1536]{1,0:T(8,128)(2,1)} %reshape.616) | copy-start | bytes 4718596
  1004.4 337.3 %reduce-scatter.5.cloned.1.call-start = ((), (), s32[]{:S(2)}) async-start(), calls=%async_computation.7 | async-start | bytes 17825792 | tf_op jit(solution)/shard_map/reduce_scatter | solution.py:158
  1011.5 98.8 %copy-start.47 = (bf16[16,32,128]{2,1,0:T(8,128)(2,1)}, bf16[16,32,128]{2,1,0:T(8,128)(2,1)S(1)}, u32[]{:S(2)}) copy-start(bf16[16,32,128]{2,1,0:T(8,128)(2,1)S(1)} %fusion.24) | copy-start | bytes 393220
  1011.5 98.8 %copy-start.82 = (f32[128]{0:T(128)S(1)}, f32[128]{0:T(128)}, u32[]{:S(2)}) copy-start(f32[128]{0:T(128)} %get-tuple-element.44) | copy-start | bytes 1540
  1111.5 14.5 copy-start.33
  1163.1 2080.4 %all-reduce.7.cloned.1.call-start = ((), (), s32[]{:S(2)}) async-start(), calls=%async_computation.10 | async-start | bytes 140410880
  1218.6 124.4 %copy-start.6 = (f32[128,1024]{1,0:T(8,128)S(1)}, f32[128,1024]{1,0:T(8,128)}, u32[]{:S(2)}) copy-start(f32[128,1024]{1,0:T(8,128)} %copy-done.5) | copy-start | bytes 1572868
  1218.6 124.4 %copy-start.54 = (f32[1024]{0:T(1024)S(1)}, f32[1024]{0:T(1024)}, u32[]{:S(2)}) copy-start(f32[1024]{0:T(1024)} %copy-done.53) | copy-start | bytes 12292
  1218.6 124.4 %copy-start.56 = (f32[1024]{0:T(1024)S(1)}, f32[1024]{0:T(1024)}, u32[]{:S(2)}) copy-start(f32[1024]{0:T(1024)} %copy-done.55) | copy-start | bytes 12292
  1218.6 124.4 %copy-start.75 = (f32[128]{0:T(128)S(1)}, f32[128]{0:T(128)}, u32[]{:S(2)}) copy-start(f32[128]{0:T(128)} %copy-done.74) | copy-start | bytes 1540
  1218.6 124.4 %copy-start.77 = (f32[128]{0:T(128)S(1)}, f32[128]{0:T(128)}, u32[]{:S(2)}) copy-start(f32[128]{0:T(128)} %copy-done.76) | copy-start | bytes 1540
  2104.9 1257.1 %all-reduce.5.cloned.1.call-start = ((), (), s32[]{:S(2)}) async-start(), calls=%async_computation.8 | async-start | bytes 8775680 | tf_op jit(solution)/shard_map/psum | solution.py:351
  3250.1 186.8 %copy-start.25 = (f32[548480]{0:T(1024)S(1)}, f32[548480]{0:T(1024)}, u32[]{:S(2)}) copy-start(f32[548480]{0:T(1024)} %param.16) | copy-start | bytes 6581764
  3412.9 24.0 copy-start.9
  3412.9 24.0 copy-start.24
  (90 other events, 480.0 us)
Sparse Core Ops, SparseCore 0:
  22.4 373.7 all-gather.15
  728.6 48.7 all-gather.7
  779.5 49.0 all-gather.9
  861.6 39.8 all-gather.11
  903.5 40.1 all-gather.13
  1004.5 103.5 reduce-scatter.2
  1163.3 178.3 reduce-scatter.4
  2105.1 1138.4 all-reduce.6
  3250.3 111.6 all-reduce.4
where the time goes:
time: 3490 us; the launch traced here: 3450 us
  waiting for transfers between devices  1850 us (53%)
  local copies, waits for them, and re-layouts  1010 us (29%)
  other arithmetic  329 us (9%)
  matrix products  173 us (5%)
  blocking collectives  63.1 us (2%)
    unnamed x10, waiting for transfers between devices  1140 us
    concatenate x1, local copies, waits for them, and re-layouts, body(): jnp.concatenate([g.reshape(-1) for g in grads] + [jnp.zeros((total_params...  546 us
    all_gather x1, waiting for transfers between devices, body(): lax.all_gather(master.astype(jnp.bfloat16), ('dp', 'seq'), axis=0, tiled=...  345 us
    all_gather x1, other arithmetic, body(): lax.all_gather(master.astype(jnp.bfloat16), ('dp', 'seq'), axis=0, tiled=...  220 us
    reduce_scatter x2, waiting for transfers between devices, attend_back(): lax.psum_scatter(jnp.concatenate([grad_keys.reshape(count, -1), grad_valu...  217 us
    reshape x2, local copies, waits for them, and re-layouts, body(): grad_flat.reshape(groups, seqs, shard)  181 us
    unnamed x235, local copies, waits for them, and re-layouts  159 us
    psum x1, waiting for transfers between devices, body(): summed = lax.psum(partial_share, 'dp')  110 us
  transfers between devices with their start and end apart: 9, of which 8 were waited for; matrix products, arithmetic and copies ran while one was open for 6% of the time, Pallas kernels for 0%

commit v1 on v0

--- a/solution.py
+++ b/solution.py
@@ -1,8 +1,11 @@
+import functools
 import math
 
 import jax
 import jax.numpy as jnp
 from jax import lax
+from jax.experimental import pallas as pl
+from jax.experimental.pallas import tpu as pltpu
 from jax.sharding import PartitionSpec as P
 
 D = 1024
@@ -123,108 +126,240 @@
     ) * 0.25
 
 
-def masked_scores(queries, keys, query_image, key_image, key_seen, scale):
-    raw = jnp.einsum("rhd,khd->hrk", queries, keys, preferred_element_type=jnp.float32) * scale
-    allowed = (query_image[:, None] == key_image[None, :]) & (key_seen[None, :] > 0)
-    return jnp.where(allowed[None], raw, -1e30)
-
-
-def attend(queries, keys, values, key_seen, query_image, key_image, scale):
-    scores = masked_scores(queries, keys, query_image, key_image, key_seen, scale)
-    top = jnp.max(scores, axis=-1)
-    mass = jnp.sum(jnp.where(scores > -1e29, jnp.exp(scores - top[..., None]), 0.0), axis=-1)
-    lse = top + jnp.log(mass)
-    probs = jnp.exp(scores - lse[..., None]).astype(jnp.bfloat16)
-    out = jnp.einsum("hrk,khd->rhd", probs, values, preferred_element_type=jnp.float32)
-    return (out, lse)
-
-
-def attend_back(queries, keys, values, key_seen, query_image, key_image, out, lse, grad_out, scale):
-    rows, heads, depth = queries.shape
-    dterm = jnp.transpose(jnp.sum(grad_out.astype(jnp.float32) * out, axis=-1))
-    scores = masked_scores(queries, keys, query_image, key_image, key_seen, scale)
-    probs = jnp.exp(scores - lse[..., None])
-    dprob = jnp.einsum("rhd,khd->hrk", grad_out, values, preferred_element_type=jnp.float32)
-    dscore = (probs * (dprob - dterm[..., None])).astype(jnp.bfloat16)
-    probs_low = probs.astype(jnp.bfloat16)
-    grad_queries = jnp.einsum("hrk,khd->rhd", dscore, keys, preferred_element_type=jnp.float32)
-    count = rows * lax.axis_size("seq")
-    grad_keys = (
-        jnp.einsum("hrk,rhd->khd", dscore, queries, preferred_element_type=jnp.float32) * scale
-    )
-    grad_values = jnp.einsum(
-        "hrk,rhd->khd", probs_low, grad_out, preferred_element_type=jnp.float32
-    )
-    grad_kv = lax.psum_scatter(
-        jnp.concatenate([grad_keys.reshape(count, -1), grad_values.reshape(count, -1)], axis=1),
-        "seq",
-        scatter_dimension=0,
-        tiled=True,
-    )
-    return (grad_queries * scale, grad_kv)
-
-
-def block_forward(x, weights, seen, query_image, key_image, heads):
+MESH = pl.DeviceIdType.MESH
+NEG = -1e30
+QB = 256
+KB = 256
+
+
+def swap_kernel(n, x_ref, o_ref, send_sem, recv_sem, own_sem):
+    me = lax.axis_index("seq")
+    barrier = pltpu.get_barrier_semaphore()
+    for k in range(1, n):
+        pl.semaphore_signal(
+            barrier, inc=1, device_id={"seq": lax.rem(me + k, n)}, device_id_type=MESH
+        )
+    pl.semaphore_wait(barrier, n - 1)
+    copies = []
+    for k in range(1, n):
+        peer = lax.rem(me + k, n)
+        copy = pltpu.make_async_remote_copy(
+            src_ref=x_ref.at[peer],
+            dst_ref=o_ref.at[me],
+            send_sem=send_sem.at[k],
+            recv_sem=recv_sem.at[k],
+            device_id={"seq": peer},
+            device_id_type=MESH,
+        )
+        copy.start()
+        copies.append(copy)
+    own = pltpu.make_async_copy(x_ref.at[me], o_ref.at[me], own_sem)
+    own.start()
+    own.wait()
+    for copy in copies:
+        copy.wait()
+
+
+def swap(x, collective):
+    n = x.shape[0]
+    return pl.pallas_call(
+        functools.partial(swap_kernel, n),
+        out_shape=jax.ShapeDtypeStruct(x.shape, x.dtype),
+        in_specs=[pl.BlockSpec(memory_space=pltpu.VMEM)],
+        out_specs=pl.BlockSpec(memory_space=pltpu.VMEM),
+        scratch_shapes=[
+            pltpu.SemaphoreType.DMA((n,)),
+            pltpu.SemaphoreType.DMA((n,)),
+            pltpu.SemaphoreType.DMA,
+        ],
+        compiler_params=pltpu.CompilerParams(collective_id=collective, has_side_effects=True),
+        name="swap%d" % collective,
+    )(x)
+
+
+def dot_tn(a, b):
+    return lax.dot_general(a, b, (((0,), (0,)), ((), ())), preferred_element_type=jnp.float32)
+
+
+def dot_nt(a, b):
+    return lax.dot_general(a, b, (((1,), (1,)), ((), ())), preferred_element_type=jnp.float32)
+
+
+def spread(x_ref, wide_ref):
+    for s in range(x_ref.shape[0]):
+        wide_ref[:, s * x_ref.shape[2] : (s + 1) * x_ref.shape[2]] = x_ref[s]
+
+
+def scores_of(wide_ref, depth, aux, query, kb, first, last, scale):
+    keys = wide_ref[2 * depth : 3 * depth + aux, pl.ds(pl.multiple_of(kb * KB, KB), KB)]
+    raw = dot_tn(keys, query) * scale
+    index = kb * KB + lax.broadcasted_iota(jnp.int32, raw.shape, 0)
+    return jnp.where((index >= first) & (index < last), raw, NEG)
+
+
+def query_of(wide_ref, depth, aux, qb):
+    query = wide_ref[0:depth, qb * QB : (qb + 1) * QB]
+    if aux:
+        ones = (lax.broadcasted_iota(jnp.int32, (aux, QB), 0) == 0).astype(jnp.bfloat16)
+        query = jnp.concatenate([query, ones], axis=0)
+    return query
+
+
+def attend_kernel(depth, aux, span_ref, x_ref, first_ref, last_ref, out_ref, full_ref, lse_ref, wide_ref, s_ref):
+    total = wide_ref.shape[1]
+    scale = depth ** (-0.5)
+    tokens = x_ref.shape[2]
+    spread(x_ref, wide_ref)
+    for qb in range(total // QB):
+        at = slice(qb * QB, (qb + 1) * QB)
+        query = query_of(wide_ref, depth, aux, qb)
+        first, last = first_ref[:, at], last_ref[:, at]
+        low, high = span_ref[0, qb], span_ref[1, qb]
+
+        def score(kb, top):
+            s = scores_of(wide_ref, depth, aux, query, kb, first, last, scale)
+            s_ref[pl.ds(pl.multiple_of(kb * KB, KB), KB), :] = s
+            return jnp.maximum(top, jnp.max(s, axis=0, keepdims=True))
+
+        top = lax.fori_loop(low, high, score, jnp.full((1, QB), NEG, jnp.float32))
+
+        def weigh(kb, mass):
+            rows = pl.ds(pl.multiple_of(kb * KB, KB), KB)
+            p = jnp.exp(s_ref[rows, :] - top)
+            s_ref[rows, :] = p
+            return mass + jnp.sum(p, axis=0, keepdims=True)
+
+        mass = lax.fori_loop(low, high, weigh, jnp.zeros((1, QB), jnp.float32))
+        inverse = 1.0 / mass
+
+        def gather(kb, total_out):
+            rows = pl.ds(pl.multiple_of(kb * KB, KB), KB)
+            p = (s_ref[rows, :] * inverse).astype(jnp.bfloat16)
+            values = wide_ref[depth : 2 * depth, rows]
+            return total_out + jnp.dot(values, p, preferred_element_type=jnp.float32)
+
+        out = lax.fori_loop(low, high, gather, jnp.zeros((depth, QB), jnp.float32))
+        full_ref[:, at] = out
+        lse_ref[:, at] = top + jnp.log(mass)
+        for part in range(QB // tokens):
+            out_ref[qb * (QB // tokens) + part] = out[:, part * tokens : (part + 1) * tokens].astype(jnp.bfloat16)
+
+
+def attend_back_kernel(
+    depth, aux, span_ref, x_ref, g_ref, first_ref, last_ref, full_ref, lse_ref, out_ref, wide_ref, gwide_ref, dq_ref, dk_ref, dv_ref
+):
+    total = wide_ref.shape[1]
+    scale = depth ** (-0.5)
+    tokens = x_ref.shape[2]
+    spread(x_ref, wide_ref)
+    spread(g_ref, gwide_ref)
+    dk_ref[...] = jnp.zeros_like(dk_ref)
+    dv_ref[...] = jnp.zeros_like(dv_ref)
+    for qb in range(total // QB):
+        at = slice(qb * QB, (qb + 1) * QB)
+        query = query_of(wide_ref, depth, aux, qb)
+        plain = wide_ref[0:depth, at]
+        first, last = first_ref[:, at], last_ref[:, at]
+        grad = gwide_ref[:, at]
+        lse = lse_ref[:, at]
+        dterm = jnp.sum(grad.astype(jnp.float32) * full_ref[:, at], axis=0, keepdims=True)
+        low, high = span_ref[0, qb], span_ref[1, qb]
+
+        def step(kb, dq):
+            rows = pl.ds(pl.multiple_of(kb * KB, KB), KB)
+            s = scores_of(wide_ref, depth, aux, query, kb, first, last, scale)
+            p = jnp.exp(s - lse)
+            dp = dot_tn(wide_ref[depth : 2 * depth, rows], grad)
+            ds = (p * (dp - dterm)).astype(jnp.bfloat16)
+            dk_ref[:, rows] += dot_nt(plain, ds)
+            dv_ref[:, rows] += dot_nt(grad, p.astype(jnp.bfloat16))
+            return dq + jnp.dot(wide_ref[2 * depth : 3 * depth, rows], ds, preferred_element_type=jnp.float32)
+
+        dq_ref[:, at] = lax.fori_loop(low, high, step, jnp.zeros((depth, QB), jnp.float32))
+    for s in range(x_ref.shape[0]):
+        at = slice(s * tokens, (s + 1) * tokens)
+        out_ref[s, 0:depth, :] = (dq_ref[:, at] * scale).astype(jnp.bfloat16)
+        out_ref[s, depth : 2 * depth, :] = dv_ref[:, at].astype(jnp.bfloat16)
+        out_ref[s, 2 * depth : 3 * depth, :] = (dk_ref[:, at] * scale).astype(jnp.bfloat16)
+
+
+def vmem_specs(count):
+    return [pl.BlockSpec(memory_space=pltpu.VMEM)] * count
+
+
+def attend(x, spans, first, last, depth, aux):
+    n, rows, tokens = x.shape
+    total = n * tokens
+    return pl.pallas_call(
+        functools.partial(attend_kernel, depth, aux),
+        out_shape=(
+            jax.ShapeDtypeStruct((n, depth, tokens), jnp.bfloat16),
+            jax.ShapeDtypeStruct((depth, total), jnp.float32),
+            jax.ShapeDtypeStruct((1, total), jnp.float32),
+        ),
+        in_specs=[pl.BlockSpec(memory_space=pltpu.SMEM)] + vmem_specs(3),
+        out_specs=tuple(vmem_specs(3)),
+        scratch_shapes=[pltpu.VMEM((rows, total), jnp.bfloat16), pltpu.VMEM((total, QB), jnp.float32)],
+        name="attend%d" % depth,
+    )(spans, x, first, last)
+
+
+def attend_back(x, grad, spans, first, last, full, lse, depth, aux):
+    n, rows, tokens = x.shape
+    total = n * tokens
+    return pl.pallas_call(
+        functools.partial(attend_back_kernel, depth, aux),
+        out_shape=jax.ShapeDtypeStruct((n, 3 * depth, tokens), jnp.bfloat16),
+        in_specs=[pl.BlockSpec(memory_space=pltpu.SMEM)] + vmem_specs(6),
+        out_specs=vmem_specs(1)[0],
+        scratch_shapes=[
+            pltpu.VMEM((rows, total), jnp.bfloat16),
+            pltpu.VMEM((depth, total), jnp.bfloat16),
+            pltpu.VMEM((depth, total), jnp.float32),
+            pltpu.VMEM((depth, total), jnp.float32),
+            pltpu.VMEM((depth, total), jnp.float32),
+        ],
+        name="attend_back%d" % depth,
+    )(spans, x, grad, first, last, full, lse)
+
+
+def block_forward(x, weights, hide, where, heads, collective):
     norms, qkv_w, out_w, out_b, up_w, up_b, down_w, down_b = weights
+    spans, first, last = where
     gains = norms.astype(jnp.float32)
     rows, width = x.shape
     depth = width // heads
-    scale = depth ** (-0.5)
     normed = layer_norm(x, gains[0], gains[1]).astype(jnp.bfloat16)
-    mixed = matmul(normed, qkv_w).astype(jnp.bfloat16)
-    queries = mixed[:, :width].reshape(rows, heads, depth)
-    all_keys, all_values, all_seen = (
-        lax.all_gather(mixed[:, width : 2 * width], "seq", axis=0, tiled=True),
-        lax.all_gather(mixed[:, 2 * width :], "seq", axis=0, tiled=True),
-        lax.all_gather(seen, "seq", axis=0, tiled=True),
-    )
-    all_keys = all_keys.reshape(-1, heads, depth)
-    all_values = all_values.reshape(-1, heads, depth)
-    out, lse = attend(queries, all_keys, all_values, all_seen, query_image, key_image, scale)
-    attended = out.reshape(rows, width).astype(jnp.bfloat16)
-    resid = x + matmul(attended, out_w) + out_b.astype(jnp.float32)
+    mixed = lax.dot_general(
+        qkv_w, normed, (((0,), (1,)), ((), ())), preferred_element_type=jnp.float32
+    ).astype(jnp.bfloat16)
+    mixed = mixed.reshape(3, heads, depth, rows)
+    pieces = [mixed[0], mixed[2], mixed[1]]
+    aux = 0
+    if hide is not None:
+        aux = 16
+        bias = jnp.zeros((heads, aux, rows), jnp.bfloat16).at[:, 0, :].set(hide.astype(jnp.bfloat16))
+        pieces.append(bias)
+    shared = swap(jnp.concatenate(pieces, axis=1), collective)
+    out, full, lse = attend(shared, spans, first, last, depth, aux)
+    attended = swap(out, collective + 1).reshape(width, rows)
+    resid = x + dot_tn(attended, out_w) + out_b.astype(jnp.float32)
     normed_two = layer_norm(resid, gains[2], gains[3]).astype(jnp.bfloat16)
     pre = matmul(normed_two, up_w) + up_b.astype(jnp.float32)
     hidden_act = jax.nn.gelu(pre, approximate=False).astype(jnp.bfloat16)
     result = resid + matmul(hidden_act, down_w) + down_b.astype(jnp.float32)
-    kept = (
-        x,
-        normed,
-        queries,
-        all_keys,
-        all_values,
-        all_seen,
-        out,
-        lse,
-        attended,
-        resid,
-        normed_two,
-        pre,
-        hidden_act,
-    )
+    kept = (x, normed, shared, full, lse, attended, resid, normed_two, pre, hidden_act)
     return (result, kept)
 
 
-def block_backward(grad, weights, kept, query_image, key_image, heads):
+def block_backward(grad, weights, kept, where, heads, collective):
     norms, qkv_w, out_w, out_b, up_w, up_b, down_w, down_b = weights
+    spans, first, last = where
     gains = norms.astype(jnp.float32)
-    (
-        x,
-        normed,
-        queries,
-        all_keys,
-        all_values,
-        all_seen,
-        out,
-        lse,
-        attended,
-        resid,
-        normed_two,
-        pre,
-        hidden_act,
-    ) = kept
+    x, normed, shared, full, lse, attended, resid, normed_two, pre, hidden_act = kept
     rows, width = x.shape
     depth = width // heads
+    aux = shared.shape[1] - 3 * depth
     grad_low = grad.astype(jnp.bfloat16)
     grad_down = outer(hidden_act, grad_low)
     grad_down_b = jnp.sum(grad, axis=0)
@@ -237,32 +372,37 @@
     grad_resid, grad_gain_two, grad_shift_two = norm_two_back(back_mul(pre_low, up_w))
     grad_resid = grad_resid + grad
     resid_low = grad_resid.astype(jnp.bfloat16)
-    grad_out = outer(attended, resid_low)
+    grad_out = matmul(attended, resid_low)
     grad_out_b = jnp.sum(grad_resid, axis=0)
-    grad_attended = back_mul(resid_low, out_w).astype(jnp.bfloat16).reshape(rows, heads, depth)
-    grad_queries, grad_kv = attend_back(
-        queries,
-        all_keys,
-        all_values,
-        all_seen,
-        query_image,
-        key_image,
-        out,
-        lse,
-        grad_attended,
-        depth ** (-0.5),
-    )
-    mixed_low = jnp.concatenate([grad_queries.reshape(rows, width), grad_kv], axis=1).astype(
-        jnp.bfloat16
-    )
-    grad_qkv = outer(normed, mixed_low)
+    grad_attended = back_mul(out_w, resid_low).astype(jnp.bfloat16)
+    grad_attended = swap(grad_attended.reshape(heads, depth, rows), collective + 1)
+    back = attend_back(shared, grad_attended, spans, first, last, full, lse, depth, aux)
+    back = swap(back, collective + 2).reshape(heads, 3, depth, rows)
+    mixed_low = jnp.stack([back[:, 0], back[:, 2], back[:, 1]]).reshape(3 * width, rows)
+    grad_qkv = lax.dot_general(
+        normed, mixed_low, (((0,), (1,)), ((), ())), preferred_element_type=jnp.float32
+    )
     _, norm_one_back = jax.vjp(layer_norm, x, gains[0], gains[1])
-    grad_x, grad_gain_one, grad_shift_one = norm_one_back(back_mul(mixed_low, qkv_w))
+    grad_x, grad_gain_one, grad_shift_one = norm_one_back(
+        lax.dot_general(mixed_low, qkv_w, (((0,), (1,)), ((), ())), preferred_element_type=jnp.float32)
+    )
     grad_norms = jnp.stack([grad_gain_one, grad_shift_one, grad_gain_two, grad_shift_two])
     return (
         grad_x + grad_resid,
         [grad_norms, grad_qkv, grad_out, grad_out_b, grad_up, grad_up_b, grad_down, grad_down_b],
     )
+
+
+def reach(counts, total):
+    ends = jnp.cumsum(counts)
+    starts = ends - counts
+    places = jnp.arange(total, dtype=jnp.int32)
+    inside = ((places[:, None] >= starts[None, :]) & (places[:, None] < ends[None, :])).astype(jnp.int32)
+    first = jnp.sum(inside * starts[None, :], axis=1)
+    last = jnp.sum(inside * ends[None, :], axis=1)
+    low = first[::QB] // KB
+    high = (last[QB - 1 :: QB] + KB - 1) // KB
+    return (jnp.stack([low, high]), first[None, :], last[None, :])
 
 
 def body(pixels, mask, image_count, image_width, gsd_index, step, master, moment_one, moment_two):
@@ -272,8 +412,8 @@
     group_rows = rows * lax.axis_size("seq")
     places = lax.axis_index("seq") * rows + jnp.arange(rows, dtype=jnp.int32)
     counts, widths, ground = (image_count[0], image_width[0], gsd_index[0])
-    query_image, local, row_pos, col_pos = geometry(counts, widths, ground, places)
-    key_image = geometry(counts, widths, ground, jnp.arange(group_rows, dtype=jnp.int32))[0]
+    _, local, row_pos, col_pos = geometry(counts, widths, ground, places)
+    where = reach(counts, group_rows)
     hidden = ((mask == 1) & (local != 0)).astype(jnp.float32)
     count_local = jnp.sum(hidden)
     count = lax.psum(count_local, ("dp", "seq"))
@@ -283,7 +423,7 @@
         + position_code(row_pos, col_pos, D)
     )
     encoded, enc_kept = block_forward(
-        embedded, weights[2:10], (1.0 - hidden).astype(jnp.bfloat16), query_image, key_image, HEADS
+        embedded, weights[2:10], hidden * NEG, where, HEADS, 0
     )
     encoded_low = encoded.astype(jnp.bfloat16)
     projected = matmul(encoded_low, weights[10]) + weights[11].astype(jnp.float32)
@@ -291,7 +431,7 @@
         hidden[:, None] > 0, weights[12].astype(jnp.float32)[None, :], projected
     ) + position_code(row_pos, col_pos, DD)
     decoded, dec_kept = block_forward(
-        dec_in, weights[13:21], jnp.ones((rows,), jnp.bfloat16), query_image, key_image, DHEADS
+        dec_in, weights[13:21], None, where, DHEADS, 3
     )
     decoded_low = decoded.astype(jnp.bfloat16)
     high = matmul(decoded_low, weights[21]) + weights[22].astype(jnp.float32)
@@ -317,14 +457,14 @@
     lowband_low = grad_low_pred.astype(jnp.bfloat16)
     grad_decoded = back_mul(high_low, weights[21]) + back_mul(lowband_low, weights[23])
     grad_dec_in, dec_grads = block_backward(
-        grad_decoded, weights[13:21], dec_kept, query_image, key_image, DHEADS
+        grad_decoded, weights[13:21], dec_kept, where, DHEADS, 3
     )
     grad_token = jnp.sum(hidden[:, None] * grad_dec_in, axis=0)
     grad_projected = grad_dec_in * (1.0 - hidden)[:, None]
     projected_low = grad_projected.astype(jnp.bfloat16)
     grad_encoded = back_mul(projected_low, weights[10])
     grad_embedded, enc_grads = block_backward(
-        grad_encoded, weights[2:10], enc_kept, query_image, key_image, HEADS
+        grad_encoded, weights[2:10], enc_kept, where, HEADS, 0
     )
     grads = (
         [outer(pixels, grad_embedded.astype(jnp.bfloat16)), jnp.sum(grad_embedded, axis=0)]

time: 3490 us -> 3280 us (0.940)
  waiting for transfers between devices: 1850 us -> 1620 us
  Pallas kernels: 0 us -> 188 us
  matrix products: 173 us -> 96.4 us
  other arithmetic: 329 us -> 276 us
    reduce_scatter x2 -> x0, waiting for transfers between devices: 217 us -> none  [attend_back(): lax.psum_scatter(jnp.concatenate([grad_keys.reshape(count, -1), grad_valu...]
    pallas_call x0 -> x12, Pallas kernels: none -> 188 us  [the longest x8 117 us: swap(): pl.pallas_call(functools.partial(swap_kernel, n), out_shape=jax.ShapeDtyp...]
    dot_general x12 -> x8, matrix products: 101 us -> 21.5 us  [the longest x2 8.78 us: block_backward(): lax.dot_general(normed, mixed_low, (((0,), (1,)), ((), ())), preferred_el...]
    all_gather x4 -> x0, waiting for transfers between devices: 41.3 us -> none  [the longest x2 25.4 us: block_forward(): lax.all_gather(mixed[:, width:2 * width], 'seq', axis=0, tiled=True)]
    unnamed x235 -> x177, local copies, waits for them, and re-layouts: 159 us -> 173 us
    unnamed x10 -> x4, waiting for transfers between devices: 1140 us -> 1150 us
  transfers between devices with their start and end apart: 9 -> 3, of which waited for: 8 -> 3; matrix products, arithmetic and copies ran while one was open for 6% -> 0% of each run, Pallas kernels for 0% -> 0%
where the time goes in v1:
time: 3280 us; the launch traced here: 3250 us
  waiting for transfers between devices  1620 us (49%)
  local copies, waits for them, and re-layouts  1000 us (30%)
  other arithmetic  276 us (8%)
  Pallas kernels  188 us (6%)
  matrix products  96.4 us (3%)
  blocking collectives  39.7 us (1%)
    unnamed x4, waiting for transfers between devices  1150 us
    concatenate x1, local copies, waits for them, and re-layouts, body(): jnp.concatenate([g.reshape(-1) for g in grads] + [jnp.zeros((total_params...  546 us
    all_gather x1, waiting for transfers between devices, body(): lax.all_gather(master.astype(jnp.bfloat16), ('dp', 'seq'), axis=0, tiled=...  367 us
    all_gather x1, other arithmetic, body(): lax.all_gather(master.astype(jnp.bfloat16), ('dp', 'seq'), axis=0, tiled=...  220 us
    reshape x2, local copies, waits for them, and re-layouts, body(): grad_flat.reshape(groups, seqs, shard)  181 us
    unnamed x177, local copies, waits for them, and re-layouts  173 us
    pallas_call x8, Pallas kernels, swap(): pl.pallas_call(functools.partial(swap_kernel, n), out_shape=jax.ShapeDtyp...  117 us
    psum x1, waiting for transfers between devices, body(): summed = lax.psum(partial_share, 'dp')  110 us
  transfers between devices with their start and end apart: 3, of which 3 were waited for; matrix products, arithmetic and copies ran while one was open for 0% of the time, Pallas kernels for 0%

profile of v1, /device:TPU:0, one launch (start us, length us, event | category | flops | bytes accessed | tf_op | source)
XLA Modules:
  0.0 3245.7 jit_solution(12377475857537514525)
XLA Ops:
  9.0 13.2 reshape.587
  29.7 366.5 %all-gather.3.cloned.1.call-done = bf16[32,1,548480]{2,1,0:T(2,128)(2,1)} async-done(((bf16[1,1,548480]{2,1,0:T(2,128)(2,1)}), bf16[32,1,548480]{2,1,0:T(2,128)(2,1)}) %all-gather.3.cloned.1.call-update) | async-done | bytes 35102736 | tf_op jit(solution)/shard_map/all_gather | solution.py:409
  396.2 220.1 %reduce.3 = bf16[32,548480]{1,0:T(8,128)(2,1)} reduce(bf16[32,1,548480]{2,1,0:T(2,128)(2,1)} %all-gather.3.cloned.1.call-done, bf16[]{:T(256)} %constant.326), dimensions={1}, to_apply=%all-gather.reduce_sub_computation | reduce | bytes 70205440 | tf_op jit(solution)/shard_map/all_gather | solution.py:409
  616.4 92.9 %reshape.588 = bf16[17551360]{0:T(1024)(128)(2,1)} reshape(bf16[32,548480]{1,0:T(8,128)(2,1)} %reduce.3) | data formatting | bytes 70205440
  729.1 13.2 fusion.119
  752.1 10.3 reshape.548
  767.8 19.1 swap0.1.x_ref
  786.9 17.7 attend64.1
  804.6 15.0 swap1.2
  824.3 13.3 reshape.550
  837.6 13.4 slice.275
  871.8 14.4 swap3.1.x_ref
  886.2 17.6 attend32.1
  903.8 10.9 swap4.2
  953.7 9.6 swap4.3.g_ref
  963.3 17.6 attend_back32.1.x_ref
  980.9 13.7 swap5.1
  1002.7 9.8 convolution_bitcast_fusion
  1012.5 8.1 fusion.129
  1020.6 8.2 convolution_bitcast_fusion.1
  1037.1 12.8 swap1.3.g_ref
  1050.0 18.6 attend_back64.1.x_ref
  1068.6 21.2 swap2.1
  1121.1 15.1 copy.94
  1146.3 12.2 copy.91
  1166.0 545.5 %concatenate.21 = f32[17551360]{0:T(1024)} concatenate(f32[786432]{0:T(1024)} %bitcast.171, f32[1024]{0:T(1024)} %get-tuple-element.38, f32[4096]{0:T(1024)S(1)} %bitcast.202, f32[3145728]{0:T(1024)} %bitcast.166, f32[1048576]{0:T(1024)} %bitcast.169, f32[1024]{0:T(1024)} %get-tuple-element.37, f32[4194304]{0:T(1024)} %bitcast.161, f32[4096]{0:T(1024)} %get-tuple-element.150, ...), dimensions={0} | concatenate | bytes 140410880 | tf_op jit(solution)/shard_map/concatenate | solution.py:485
  1711.5 68.1 %reshape.584 = f32[2,16,548480]{2,1,0:T(8,128)} reshape(f32[17551360]{0:T(1024)} %concatenate.21) | data formatting | bytes 140410880 | tf_op jit(solution)/shard_map/reshape | solution.py:489
  1779.5 112.9 %copy.83 = f32[2,16,548480]{2,0,1:T(2,128)} copy(f32[2,16,548480]{2,1,0:T(8,128)} %reshape.584) | data formatting | bytes 140410880 | tf_op jit(solution)/shard_map/reshape | solution.py:489
  1893.7 1145.7 %all-reduce.8.cloned.1.call-done = f32[2,16,548480]{2,0,1:T(2,128)} async-done(((f32[2,16,548480]{2,0,1:T(2,128)}), f32[2,16,548480]{2,0,1:T(2,128)}) %all-reduce.8.cloned.1.call-update) | async-done | bytes 70205456
  3047.7 110.4 %all-reduce.6.cloned.1.call-done = f32[2,1,548480]{2,0,1:T(2,128)} async-done(((f32[2,1,548480]{2,0,1:T(2,128)}), f32[2,1,548480]{2,0,1:T(2,128)}) %all-reduce.6.cloned.1.call-update) | async-done | bytes 4387856 | tf_op jit(solution)/shard_map/psum | solution.py:491
  3164.9 39.7 %all-reduce.2 = (f32[]{:T(128)}, f32[]{:T(128)}, f32[]{:T(128)}) all-reduce(f32[]{:T(128)} %get-tuple-element.55, f32[]{:T(128)} %multiply_reduce_fusion.1, f32[]{:T(128)} %get-tuple-element.54), channel_id=1, replica_groups=mesh['dp'=2,'seq'=16] {'dp','seq'}, use_global_device_ids=true, to_apply=%region_44.45 | all-reduce | flops 3 | bytes 24 | tf_op jit(solution)/shard_map/psum | solution.py:419
  3208.7 24.0 multiply_reduce_fusion
  (318 shorter events, 192.8 us)
Async XLA Ops:
  7.2 389.1 %all-gather.3.cloned.1.call-start = ((), (), s32[]{:S(2)}) async-start(), calls=%async_computation.1 | async-start | bytes 72399360 | tf_op jit(solution)/shard_map/all_gather | solution.py:409
  8.9 13.4 copy-start.57
  9.0 14.5 copy-start.55
  9.0 14.5 copy-start.56
  9.0 14.7 copy-start.52
  22.3 3017.1 %all-reduce.8.cloned.1.call-start = ((), (), s32[]{:S(2)}) async-start(), calls=%async_computation.2 | async-start | bytes 140410880
  22.6 593.7 %copy-start.32 = (s32[2048]{0:T(1024)}, s32[2048]{0:T(1024)S(1)}, u32[]{:S(2)}) copy-start(s32[2048]{0:T(1024)S(1)} %get-tuple-element.52) | copy-start | bytes 24580
  22.7 593.7 %copy-start.33 = (s32[2048]{0:T(1024)}, s32[2048]{0:T(1024)S(1)}, u32[]{:S(2)}) copy-start(s32[2048]{0:T(1024)S(1)} %get-tuple-element.53) | copy-start | bytes 24580
  23.5 592.9 %copy-start.43 = (s32[768]{0:T(1024)}, s32[768]{0:T(1024)S(1)}, u32[]{:S(2)}) copy-start(s32[768]{0:T(1024)S(1)} %fusion.81) | copy-start | bytes 9220
  24.2 592.1 %copy-start.47 = (pred[128]{0:T(512)(128)(4,1)}, pred[128]{0:T(512)(128)(4,1)S(1)}, u32[]{:S(2)}) copy-start(pred[128]{0:T(512)(128)(4,1)S(1)} %get-tuple-element.70) | copy-start | bytes 388
  710.5 33.9 %slice-start = ((s8[35102720]{0:T(1024)(128)(4,1)}), s8[1548288]{0:T(1024)(128)(4,1)S(1)}, s32[]{:S(2)}) async-start(s8[35102720]{0:T(1024)(128)(4,1)} %bitcast.156), calls=%async_computation.3 | async-start | bytes 3096576
  715.1 29.3 slice-start.1
  715.1 29.3 slice-start.2
  722.5 21.9 slice-start.3
  722.5 21.9 slice-start.4
  729.0 15.4 slice-start.5
  729.0 15.4 slice-start.6
  729.0 15.5 slice-start.7
  729.0 16.7 slice-start.8
  766.8 52.8 %copy-start.12 = (bf16[1048576]{0:T(1024)(128)(2,1)S(1)}, bf16[1048576]{0:T(1024)(128)(2,1)}, u32[]{:S(2)}) copy-start(bf16[1048576]{0:T(1024)(128)(2,1)} %get-tuple-element.85) | copy-start | bytes 6291460
  870.5 44.2 %slice-start.10 = ((bf16[17551360]{0:T(1024)(128)(2,1)}), bf16[262144]{0:T(1024)(128)(2,1)S(1)}, s32[]{:S(2)}) async-start(bf16[17551360]{0:T(1024)(128)(2,1)} %reshape.588), calls=%async_computation.13 | async-start | bytes 1048576 | tf_op jit(solution)/shard_map/slice | solution.py:64
  1002.7 26.1 slice-start.12
  1012.5 16.3 slice-start.13
  1068.6 28.9 slice-start.18
  1117.5 18.7 slice-start.14
  1121.1 15.1 slice-start.15
  1121.1 15.1 slice-start.16
  1121.1 15.1 slice-start.17
  1892.5 1265.6 %all-reduce.6.cloned.1.call-start = ((), (), s32[]{:S(2)}) async-start(), calls=%async_computation | async-start | bytes 8775680 | tf_op jit(solution)/shard_map/psum | solution.py:491
  3046.2 186.5 %copy-start.22 = (f32[548480]{0:T(1024)S(1)}, f32[548480]{0:T(1024)}, u32[]{:S(2)}) copy-start(f32[548480]{0:T(1024)} %param.18) | copy-start | bytes 6581764
  3208.7 24.0 copy-start.7
  3208.7 24.0 copy-start.21
  (55 other events, 227.0 us)
Sparse Core Ops, SparseCore 0:
  22.4 373.7 all-gather.2
  1892.6 1146.6 all-reduce.7
  3046.3 111.6 all-reduce.5
